TPU v7x, 512 devices: a whole 4x8x8 slice. The times are simulated.
512 devices in a mesh: pop: 32 (over z, x_lo, core), mp: 16 (over x_hi, y).
Axes of the slice: x: 4 (x_hi: 2, x_lo: 2; x = x_hi * 2 + x_lo), y: 8, z: 8, core: 2. Of those that a mesh axis runs over, the one named last changes fastest.
Arguments:
- prompts: bfloat16 [128, 128, 4096], P('pop'), may hold values from -9 to 9
- gate_weight: bfloat16 [4096, 8192], P('pop', 'mp'), may hold values from -0.09375 to 0.09375
- up_weight: bfloat16 [4096, 8192], P('pop', 'mp'), may hold values from -0.09375 to 0.09375
- reward_head: bfloat16 [8192], P('mp'), may hold values from -0.0625 to 0.0625
- member_seeds: int32 [128], P('pop'), may hold values from 0 to 1073741823
- counters: int32 [128], P('pop'), may hold values from 0 to 65535
- member_ranks: int32 [128], P('pop'), may hold values from 0 to 127, each once
Outputs:
- new_gate: bfloat16 [4096, 8192], P('pop', 'mp')
- new_up: bfloat16 [4096, 8192], P('pop', 'mp')
- scores: float32 [128], P('pop')
All inputs are finite; a program needn't handle non-finite values.
Results may differ from a plain program's by a relative error of at most 0.014.
Values may be sent and summed in bfloat16 or wider, within the bound.
A program may use at most 64 MiB of HBM per device.

v0:
```python
import jax
import jax.numpy as jnp
from jax import lax
from jax.sharding import PartitionSpec as P

sigma_perturb = 0.004
learn_rate = 0.0016


def shift_down(number, amount):
    return lax.shift_right_logical(number, jnp.full_like(number, amount))


def mix_bits(number):
    number = number ^ shift_down(number, 16)
    number = number * 2146121005
    number = number ^ shift_down(number, 15)
    number = number * -2073254261
    return number ^ shift_down(number, 16)


def factor_rows(seed_list, counter_list, slot, positions):
    anchor = mix_bits(
        seed_list * 1103515245 + mix_bits(counter_list * 668265263 + slot * 374761393)
    )
    hashed = mix_bits(anchor[:, None] + positions[None, :] * -1640531535)
    uniform_part = shift_down(hashed, 8).astype(jnp.float32) * (1.0 / 16777216.0)
    return (2.0 * uniform_part - 1.0 + 1.0 / 16777216.0) * 1.7320508075688772


def shards(prompts, gate_weight, up_weight, reward_head, member_seeds, counters, member_ranks):
    members_here, seq_len, width = prompts.shape
    own_rows, own_cols = gate_weight.shape
    pop_index = lax.axis_index("pop")
    mp_index = lax.axis_index("mp")
    row_start = pop_index * own_rows
    column_ids = mp_index * own_cols + jnp.arange(own_cols, dtype=jnp.int32)
    all_seeds, all_counters, all_ranks = (
        lax.all_gather(member_seeds, "pop", axis=0, tiled=True),
        lax.all_gather(counters, "pop", axis=0, tiled=True),
        lax.all_gather(member_ranks, "pop", axis=0, tiled=True),
    )
    members_all = all_seeds.shape[0]
    fitness = (all_ranks.astype(jnp.float32) + 0.5) / members_all - 0.5
    scaling = learn_rate / (members_all * sigma_perturb)
    right_gate = factor_rows(all_seeds, all_counters, 1, column_ids).astype(jnp.bfloat16)
    right_up = factor_rows(all_seeds, all_counters, 3, column_ids).astype(jnp.bfloat16)

    def fresh_rows(weight_rows, first_row, slot, right_factor):
        row_ids = first_row + jnp.arange(weight_rows.shape[0], dtype=jnp.int32)
        left_factor = (
            factor_rows(all_seeds, all_counters, slot, row_ids) * fitness[:, None]
        ).astype(jnp.bfloat16)
        update_term = scaling * jnp.dot(
            left_factor.T, right_factor, preferred_element_type=jnp.float32
        )
        return (weight_rows.astype(jnp.float32) + update_term).astype(jnp.bfloat16)

    new_gate = fresh_rows(gate_weight, row_start, 0, right_gate)
    new_up = fresh_rows(up_weight, row_start, 2, right_up)
    flat_rows = prompts.reshape(members_here * seq_len, width)
    gate_base = jnp.dot(
        flat_rows,
        lax.all_gather(new_gate, "pop", axis=0, tiled=True),
        preferred_element_type=jnp.float32,
    )
    up_base = jnp.dot(
        flat_rows,
        lax.all_gather(new_up, "pop", axis=0, tiled=True),
        preferred_element_type=jnp.float32,
    )
    later = counters + 1
    all_positions = jnp.arange(width, dtype=jnp.int32)
    gate_vec = factor_rows(member_seeds, later, 0, all_positions).astype(jnp.bfloat16)
    gate_col = factor_rows(member_seeds, later, 1, column_ids)
    up_vec = factor_rows(member_seeds, later, 2, all_positions).astype(jnp.bfloat16)
    up_col = factor_rows(member_seeds, later, 3, column_ids)
    gate_proj = jnp.einsum("mld,md->ml", prompts, gate_vec, preferred_element_type=jnp.float32)
    up_proj = jnp.einsum("mld,md->ml", prompts, up_vec, preferred_element_type=jnp.float32)
    gate_value = (
        gate_base.reshape(members_here, seq_len, own_cols)
        + sigma_perturb * gate_proj[:, :, None] * gate_col[:, None, :]
    )
    up_value = (
        up_base.reshape(members_here, seq_len, own_cols)
        + sigma_perturb * up_proj[:, :, None] * up_col[:, None, :]
    )
    hidden = (jax.nn.silu(gate_value) * up_value).astype(jnp.bfloat16)
    partial_reward = jnp.einsum("mlf,f->m", hidden, reward_head, preferred_element_type=jnp.float32)
    summed = lax.psum(partial_reward, "mp")
    all_rewards = lax.all_gather(summed, "pop", axis=0, tiled=True)
    rewards = all_rewards / seq_len
    reward_mean = jnp.mean(rewards)
    reward_var = jnp.mean((rewards - reward_mean) ** 2)
    all_scores = (rewards - reward_mean) / jnp.sqrt(reward_var + 1e-05)
    own_scores = lax.dynamic_slice_in_dim(all_scores, pop_index * members_here, members_here)
    return (new_gate, new_up, own_scores)


def solution(mesh):
    in_specs = (
        P("pop", None, None),
        P("pop", "mp"),
        P("pop", "mp"),
        P("mp"),
        P("pop"),
        P("pop"),
        P("pop"),
    )
    out_specs = (P("pop", "mp"), P("pop", "mp"), P("pop"))
    return jax.shard_map(shards, mesh=mesh, in_specs=in_specs, out_specs=out_specs, check_vma=False)
```

profile of v0, /device:TPU:1, one launch (start us, length us, event | category | flops | bytes accessed | tf_op | source)
XLA Modules:
  0.0 286.7 jit_solution(374049594415008718)
XLA Ops:
  7.2 0.0 all-gather.3.cloned.1.call-start
  7.2 1.3 dynamic-slice
  9.2 0.9 dynamic-update-slice
  10.0 0.8 dynamic-update-slice.1
  10.9 0.8 dynamic-update-slice.2
  11.7 20.1 %all-reduce.4 = (s32[128]{0:T(128)S(1)}, s32[128]{0:T(128)S(1)}, s32[128]{0:T(128)S(1)}) all-reduce(s32[128]{0:T(128)S(1)} %dynamic-update-slice, s32[128]{0:T(128)S(1)} %dynamic-update-slice.1, s32[128]{0:T(128)S(1)} %dynamic-update-slice.2), channel_id=1, replica_groups=mesh['pop'=32,'mp'=16] {'pop'}, use_global_device_ids=true, to_apply=%add | all-reduce | flops 384 | bytes 3072
  31.9 2.0 fusion.2
  33.9 0.0 all-gather.3.cloned.1.call-update
  33.9 0.0 all-gather.5.cloned.1.call-start
  33.9 2.0 fusion.3
  35.9 0.0 all-gather.5.cloned.1.call-update
  35.9 0.7 reshape.142
  36.6 0.0 copy-start
  36.6 0.8 shift-right-logical_xor_fusion.42
  37.4 0.2 fusion.80
  37.7 3.6 %fusion.72 = f32[4,1,128]{2,1,0:T(1,128)S(1)} fusion(bf16[4,128,4096]{2,1,0:T(8,128)(2,1)} %param.7, bf16[4,4096,1]{1,0,2:T(4,128)(2,1)S(1)} %get-tuple-element.7), kind=kOutput, calls=%fused_computation.93 | convolution fusion | flops 4194304 | bytes 4229120 | tf_op jit(solution)/shard_map/mld,md->ml/dot_general | solution.py:79
  41.2 0.0 copy-done
  41.2 1.2 fusion.74
  42.5 0.1 fusion.108
  42.6 61.3 %all-gather.3.cloned.1.call-done = bf16[4096,512]{1,0:T(8,128)(2,1)} async-done(((bf16[128,512]{1,0:T(8,128)(2,1)}), bf16[4096,512]{1,0:T(8,128)(2,1)}) %all-gather.3.cloned.1.call-update) | async-done | bytes 4194320 | tf_op jit(solution)/shard_map/all_gather | solution.py:64
  103.9 5.8 %fusion.173 = f32[512,512]{0,1:T(8,128)S(1)} fusion(bf16[512,4096]{1,0:T(8,128)(2,1)} %bitcast.28, bf16[4096,512]{1,0:T(8,128)(2,1)} %all-gather.3.cloned.1.call-done), kind=kOutput, calls=%fused_computation.259 | convolution fusion | flops 2147483648 | bytes 9437184 | tf_op jit(solution)/shard_map/dot_general | solution.py:62
  109.7 66.5 %all-gather.5.cloned.1.call-done = bf16[4096,512]{1,0:T(8,128)(2,1)} async-done(((bf16[128,512]{1,0:T(8,128)(2,1)}), bf16[4096,512]{1,0:T(8,128)(2,1)}) %all-gather.5.cloned.1.call-update) | async-done | bytes 4194320 | tf_op jit(solution)/shard_map/all_gather | solution.py:69
  176.2 6.0 %convert_reduce_fusion = bf16[4,512]{1,0:T(4,128)(2,1)S(1)} fusion(f32[4,512]{1,0:T(4,128)S(1)} %get-tuple-element.9, f32[4,128]{1,0:T(4,128)S(1)} %get-tuple-element.18, f32[4,512]{1,0:T(4,128)S(1)} %get-tuple-element.8, f32[4,128]{1,0:T(4,128)S(1)} %get-tuple-element.19, f32[512,512]{0,1:T(8,128)S(1)} %fusion.173, bf16[512,4096]{1,0:T(8,128)(2,1)} %bitcast.29, ...), kind=kOutput, calls=%fused_computation.7 | convolution fusion | flops 2150627328 | bytes 9461760 | tf_op jit(solution)/shard_map/dot_general | solution.py:67
  182.1 0.1 convolution_bitcast_fusion
  182.3 34.3 %psum.7 = f32[4]{0:T(128)S(1)} all-reduce(f32[4]{0:T(128)S(1)} %convolution_bitcast_fusion), channel_id=1, replica_groups=mesh['pop'=32,'mp'=16] {'mp'}, use_global_device_ids=true, to_apply=%region_1.2 | all-reduce | flops 4 | bytes 32 | tf_op jit(solution)/shard_map/psum | solution.py:90
  216.6 0.2 dynamic-update-slice.3
  216.8 59.9 %all-reduce.3 = f32[128]{0:T(128)S(1)} all-reduce(f32[128]{0:T(128)S(1)} %dynamic-update-slice.3), channel_id=1, replica_groups=mesh['pop'=32,'mp'=16] {'pop'}, use_global_device_ids=true, to_apply=%add.3 | all-reduce | flops 128 | bytes 1024
  276.7 0.6 fusion.156
  277.9 0.6 multiply_reduce_fusion
  279.2 0.6 dynamic_slice.3
  (11 shorter events, 0.1 us)
Async XLA Ops:
  7.2 96.7 %all-gather.3.cloned.1.call-start = ((), (), s32[]{:S(2)}) async-start(), calls=%async_computation | async-start | bytes 4325376 | tf_op jit(solution)/shard_map/all_gather | solution.py:64
  33.9 142.3 %all-gather.5.cloned.1.call-start = ((), (), s32[]{:S(2)}) async-start(), calls=%async_computation.1 | async-start | bytes 4325376 | tf_op jit(solution)/shard_map/all_gather | solution.py:69
  36.6 4.7 %copy-start = (bf16[4,128,4096]{2,1,0:T(8,128)(2,1)S(1)}, bf16[4,128,4096]{2,1,0:T(8,128)(2,1)}, u32[]{:S(2)}) copy-start(bf16[4,128,4096]{2,1,0:T(8,128)(2,1)} %param.7) | copy-start | bytes 12582916
Sparse Core Ops, SparseCore 0:
  34.0 69.8 all-gather.2
  106.6 69.5 all-gather.4
where the time goes:
time: 287 us
  waiting for transfers between devices  128 us (45%)
  blocking collectives  114 us (40%)
  matrix products  20.6 us (7%)
  between operations  16.1 us (6%)
  local copies, waits for them, and re-layouts  5.32 us (2%)
    unnamed x2, blocking collectives  80 us
    all_gather x1, waiting for transfers between devices, shards(): lax.all_gather(new_up, 'pop', axis=0, tiled=True)  66.5 us
    all_gather x1, waiting for transfers between devices, shards(): lax.all_gather(new_gate, 'pop', axis=0, tiled=True)  61.3 us
    psum x1, blocking collectives, shards(): summed = lax.psum(partial_reward, 'mp')  34.3 us
    dot_general x1, matrix products, shards(): jnp.dot(flat_rows, lax.all_gather(new_up, 'pop', axis=0, tiled=True), pre...  5.99 us
    dot_general x1, matrix products, shards(): jnp.dot(flat_rows, lax.all_gather(new_gate, 'pop', axis=0, tiled=True), p...  5.79 us
  transfers between devices with their start and end apart: 2, of which 2 were waited for; matrix products, arithmetic and copies ran while one was open for 5% of the time, Pallas kernels for 0%

commit v1 on v0

v1 whole, which is shorter than its diff:
```python
import functools

import jax
import jax.numpy as jnp
from jax import lax
from jax.experimental import pallas as pl
from jax.experimental.pallas import tpu as pltpu
from jax.sharding import PartitionSpec as P

MESH = pl.DeviceIdType.MESH
SIGMA = 0.004
RATE = 0.0016
ROOT3 = 1.7320508075688772
ZED = 8
GROUP = 16

UP_LINK = [(0, 0, 0), (0, 0, 1), (-1, 0, 0), (0, 1, 1), (-2, 0, 0), (-1, 0, 1), (-3, 0, 0), (-1, 1, 1), (-2, 0, 1), (-2, 1, 1)]
DOWN_LINK = [(-o, w, 1 - h) for o, w, h in UP_LINK]
SIDE_LINK = [(0, 0, 1), (0, 0, 0), (-1, 0, 0), (1, 0, 1), (-2, 0, 0), (2, 0, 1), (-3, 0, 0), (3, 0, 1), (-4, 0, 0), (4, 0, 1)]
SENDS = [UP_LINK, DOWN_LINK, SIDE_LINK]
ARRIVALS = [
    [(o - 1, w, h) for o, w, h in UP_LINK],
    [(o + 1, w, h) for o, w, h in DOWN_LINK],
    [(o, 1 - w, h) for o, w, h in SIDE_LINK],
]
STEPS = len(UP_LINK)


def same_piece(a, b):
    return (a[0] - b[0]) % ZED == 0 and a[1:] == b[1:]


def right_shift(v, amount):
    return lax.shift_right_logical(v, jnp.full_like(v, amount))


def mix(v):
    v = v ^ right_shift(v, 16)
    v = v * 2146121005
    v = v ^ right_shift(v, 15)
    v = v * -2073254261
    return v ^ right_shift(v, 16)


def anchor_of(seed, counter, slot):
    return mix(seed * 1103515245 + mix(counter * 668265263 + slot * 374761393))


def stream(anchor, position):
    h = mix(anchor + position * -1640531535)
    odd = (right_shift(h, 7) | 1) - 16777216
    return odd.astype(jnp.float32) * (ROOT3 / 16777216.0)


def kernel(
    mp_size, seeds, counters, ranks, prompts, gate_w, up_w, head,
    new_gate, new_up, scores,
    xall, wbuf, acc, lbuf, rbuf, vbuf, cbuf, ubuf, wown,
    s_own, s_sib, s_chip, s_all, r_own, r_sib, r_part, r_all, t_part, t_all,
    ring_s, ring_r, one_s, one_r, seed_s, seed_r, red_s, red_r, local_sem,
):
    rows, cols = gate_w.shape
    half = cols // 2
    tokens, width = prompts.shape
    members_here = seeds.shape[0]
    p = lax.axis_index("pop")
    m = lax.axis_index("mp")
    z = p // 4
    xl = lax.rem(p // 2, 2)
    c = lax.rem(p, 2)
    q = p // 2
    members_all = 128

    def pop_of(zz, xx, cc):
        return (zz * 2 + xx) * 2 + cc

    sibling = (pop_of(z, xl, 1 - c), m)
    up = (pop_of(lax.rem(z + 1, ZED), xl, c), m)
    down = (pop_of(lax.rem(z + ZED - 1, ZED), xl, c), m)
    side = (pop_of(z, 1 - xl, c), m)
    links = [up, down, side]

    def chip_peer(i):
        return (2 * lax.rem(q + i, GROUP) + c, m)

    def mp_peer(i):
        return (p, lax.rem(m + i, mp_size))

    barrier = pltpu.get_barrier_semaphore()
    pl.semaphore_signal(barrier, inc=1, device_id=sibling, device_id_type=MESH)

    def greet(i, carry):
        pl.semaphore_signal(barrier, inc=1, device_id=chip_peer(i), device_id_type=MESH)
        return carry

    def greet_mp(i, carry):
        pl.semaphore_signal(barrier, inc=1, device_id=mp_peer(i), device_id_type=MESH)
        return carry

    lax.fori_loop(1, GROUP, greet, 0)
    lax.fori_loop(1, mp_size, greet_mp, 0)

    my_cols = pl.ds(pl.multiple_of(c * half, half), half)
    sib_cols = pl.ds(pl.multiple_of((1 - c) * half, half), half)
    own_rows = pl.ds(pl.multiple_of(c * tokens, tokens), tokens)
    keep_gate = pltpu.make_async_copy(gate_w.at[:, my_cols], wbuf.at[p, :, pl.ds(0, half)], local_sem.at[0])
    keep_up = pltpu.make_async_copy(up_w.at[:, my_cols], wbuf.at[p, :, pl.ds(half, half)], local_sem.at[1])
    keep_gate.start()
    keep_up.start()
    own_prompts = pltpu.make_async_copy(prompts, xall.at[own_rows], local_sem.at[2])
    own_prompts.start()
    load_gate = pltpu.make_async_copy(gate_w, wown.at[0], local_sem.at[3])
    load_up = pltpu.make_async_copy(up_w, wown.at[1], local_sem.at[4])
    load_gate.start()
    load_up.start()

    lane = lax.broadcasted_iota(jnp.int32, (8, 128), 1)
    sub = lax.broadcasted_iota(jnp.int32, (8, 128), 0)
    block = jnp.zeros((8, 128), jnp.int32)
    for i in range(members_here):
        here = lane == p * members_here + i
        for row, values in enumerate((seeds, counters, ranks)):
            block = jnp.where(here & (sub == row), values[i], block)
    s_own[...] = block

    pl.semaphore_wait(barrier, GROUP + mp_size - 1)

    def remote(src, dst, send, recv, device):
        return pltpu.make_async_remote_copy(
            src_ref=src, dst_ref=dst, send_sem=send, recv_sem=recv, device_id=device, device_id_type=MESH
        )

    give_gate = remote(gate_w.at[:, sib_cols], wbuf.at[p, :, pl.ds(0, half)], one_s.at[0], one_r.at[0], sibling)
    give_up = remote(up_w.at[:, sib_cols], wbuf.at[p, :, pl.ds(half, half)], one_s.at[1], one_r.at[1], sibling)
    give_seeds = remote(s_own, s_sib, one_s.at[2], one_r.at[2], sibling)
    give_prompts = remote(prompts, xall.at[own_rows], one_s.at[3], one_r.at[3], sibling)
    give_gate.start()
    give_up.start()
    give_seeds.start()

    def ring_copy(link, index):
        offset, other, core = SENDS[link][index]
        column = 1 - xl if other else xl
        where = pop_of(lax.rem(z + offset + 2 * ZED, ZED), column, core)
        piece = wbuf.at[where]
        return remote(piece, piece, ring_s.at[link, index], ring_r.at[link, index], links[link])

    def pass_on(piece):
        for link in range(3):
            for index, sent in enumerate(SENDS[link]):
                if same_piece(piece, sent):
                    ring_copy(link, index).start()

    def arrive(step):
        for link in range(3):
            ring_copy(link, step).wait_recv()
            pass_on(ARRIVALS[link][step])

    keep_gate.wait()
    keep_up.wait()
    give_gate.wait_recv()
    give_up.wait_recv()
    for index in (0, 1):
        for link in range(3):
            ring_copy(link, index).start()
    give_prompts.start()

    give_seeds.wait_recv()
    s_chip[...] = s_own[...] + s_sib[...]
    s_all[q] = s_chip[...]

    def seed_copy(i):
        return remote(s_chip, s_all.at[q], seed_s.at[i], seed_r.at[i], chip_peer(i))

    def over_peers(act, count=GROUP):
        def step(i, carry):
            act(i)
            return carry

        lax.fori_loop(1, count, step, 0)

    over_peers(lambda i: seed_copy(i).start())

    acc[...] = jnp.zeros_like(acc)
    arrive(0)
    over_peers(lambda i: seed_copy(i).wait_recv())
    table = s_all[0]
    for i in range(1, GROUP):
        table = table + s_all[i]
    seed_row = table[0:1, :]
    count_row = table[1:2, :]
    fit_row = (table[2:3, :].astype(jnp.float32) + 0.5) / members_all - 0.5
    left_gate = anchor_of(seed_row, count_row, 0)
    left_up = anchor_of(seed_row, count_row, 2)
    right_gate = anchor_of(seed_row, count_row, 1)
    right_up = anchor_of(seed_row, count_row, 3)
    scaling = RATE / (members_all * SIGMA)

    def hash_left(first, count):
        def step(i, carry):
            start = pl.multiple_of(i * 128, 128)
            position = start + lax.broadcasted_iota(jnp.int32, (128, 128), 0)
            lbuf[pl.ds(start, 128), 0:128] = (stream(left_gate, position) * fit_row).astype(jnp.bfloat16)
            lbuf[pl.ds(start, 128), 128:256] = (stream(left_up, position) * fit_row).astype(jnp.bfloat16)
            return carry

        lax.fori_loop(first, first + count, step, 0)

    def hash_right():
        def step(i, carry):
            start = pl.multiple_of(i * 128, 128)
            position = m * cols + start + lax.broadcasted_iota(jnp.int32, (128, 128), 0)
            rbuf[pl.ds(start, 128), 0:128] = stream(right_gate, position).astype(jnp.bfloat16)
            rbuf[pl.ds(start, 128), 128:256] = stream(right_up, position).astype(jnp.bfloat16)
            return carry

        lax.fori_loop(0, cols // 128, step, 0)

    def fresh_rows():
        own = pl.ds(pl.multiple_of(p * rows, rows), rows)
        load_gate.wait()
        load_up.wait()
        for index, out in enumerate((new_gate, new_up)):
            part = pl.ds(index * 128, 128)
            delta = lax.dot_general(
                lbuf[own, part], rbuf[:, part], (((1,), (1,)), ((), ())), preferred_element_type=jnp.float32
            )
            out[...] = (wown[index].astype(jnp.float32) + scaling * delta).astype(out.dtype)

    def hash_members():
        pick = lane == q * 8 + sub
        columns = [
            jnp.sum(
                jnp.where(pick, anchor_of(seed_row, count_row + 1, slot), 0), axis=1, keepdims=True
            )
            for slot in range(4)
        ]
        wide = lax.broadcasted_iota(jnp.int32, (8, 1024), 1)
        for start in range(0, width, 1024):
            vbuf[0:8, start : start + 1024] = stream(columns[0], wide + start)
            vbuf[8:16, start : start + 1024] = stream(columns[2], wide + start)
        here = m * cols + c * half + lax.broadcasted_iota(jnp.int32, (8, half), 1)
        cbuf[0:8, :] = stream(columns[1], here) * SIGMA
        cbuf[8:16, :] = stream(columns[3], here) * SIGMA

    tile = 256
    n_tiles = 2 * tokens // tile

    def project():
        def step(i, carry):
            r = pl.ds(pl.multiple_of(i * tile, tile), tile)
            own = lax.dot_general(
                xall[r, :], vbuf[...].astype(jnp.bfloat16), (((1,), (1,)), ((), ())),
                preferred_element_type=jnp.float32,
            )
            ubuf[r, 0:16] = own
            return carry

        lax.fori_loop(0, n_tiles, step, 0)

    def low_rank():
        def step(i, carry):
            r = pl.ds(pl.multiple_of(i * tile, tile), tile)
            zl = jnp.dot(xall[r, :], lbuf[...], preferred_element_type=jnp.float32) * scaling
            zl = zl.astype(jnp.bfloat16)
            for index in range(2):
                part = slice(index * 128, index * 128 + 128)
                acc[r, index * half : (index + 1) * half] += lax.dot_general(
                    zl[:, part],
                    rbuf[pl.ds(pl.multiple_of(c * half, half), half), part],
                    (((1,), (1,)), ((), ())),
                    preferred_element_type=jnp.float32,
                )
            return carry

        lax.fori_loop(0, n_tiles, step, 0)

    seq = 2 * tokens // 8

    def rank_one():
        for i in range(8):
            r = slice(i * seq, (i + 1) * seq)
            for index in range(2):
                s = slice(index * half, (index + 1) * half)
                j = index * 8 + i
                acc[r, s] += ubuf[r, j : j + 1] * cbuf[j : j + 1, :]

    def multiply(offset, other, core=None):
        zz = lax.rem(z + offset + ZED, ZED)
        column = 1 - xl if other else xl
        first = pop_of(zz, column, core or 0)
        depth = rows if core is not None else 2 * rows
        k = pl.ds(pl.multiple_of(first * rows, rows), depth)
        w_of = (lambda: wbuf[first]) if core is not None else (lambda: wbuf[pl.ds(first, 2)].reshape(depth, cols))

        def step(i, carry):
            r = pl.ds(pl.multiple_of(i * tile, tile), tile)
            acc[r, :] += jnp.dot(xall[r, k], w_of(), preferred_element_type=jnp.float32)
            return carry

        lax.fori_loop(0, n_tiles, step, 0)

    hash_left(0, 8)
    arrive(1)
    hash_left(8, 10)
    own_prompts.wait()
    give_prompts.wait_recv()
    arrive(2)
    hash_left(18, 14)
    arrive(3)
    hash_right()
    fresh_rows()
    hash_members()
    arrive(4)
    low_rank()
    arrive(5)
    project()
    rank_one()
    arrive(6)
    multiply(0, 0)
    multiply(0, 1)
    multiply(-1, 0)
    multiply(1, 0)
    arrive(7)
    multiply(-1, 1)
    multiply(1, 1)
    multiply(-2, 0)
    multiply(2, 0)
    multiply(4, 0)
    arrive(8)
    multiply(-2, 1)
    multiply(2, 1)
    multiply(-3, 0)
    multiply(3, 0)
    multiply(-3, 1, 0)
    multiply(3, 1, 1)
    multiply(-4, 1, 0)
    arrive(9)
    multiply(-3, 1, 1)
    multiply(3, 1, 0)
    multiply(4, 1, 1)

    head_row = head[:, my_cols].astype(jnp.float32)
    parts = []
    for i in range(8):
        r = slice(i * seq, (i + 1) * seq)
        gate = acc[r, 0:half]
        value = gate / (1.0 + jnp.exp(-gate)) * acc[r, half:cols]
        parts.append(jnp.sum(value, axis=0, keepdims=True))
    summed = jnp.sum(jnp.concatenate(parts, axis=0) * head_row, axis=1, keepdims=True)
    r_own[...] = jnp.where(lane == q * 8 + sub, summed, 0.0)

    give_reward = remote(r_own, r_sib, one_s.at[4], one_r.at[4], sibling)
    give_reward.start()
    give_reward.wait_recv()
    r_part[...] = r_own[...] + r_sib[...]
    r_all[m] = r_part[...]

    def part_copy(i):
        return remote(r_part, r_all.at[m], red_s.at[0, i], red_r.at[0, i], mp_peer(i))

    over_peers(lambda i: part_copy(i).start(), mp_size)
    over_peers(lambda i: part_copy(i).wait_recv(), mp_size)
    t_part[...] = jnp.sum(r_all[...], axis=0)
    t_all[q] = t_part[...]

    def total_copy(i):
        return remote(t_part, t_all.at[q], red_s.at[1, i], red_r.at[1, i], chip_peer(i))

    over_peers(lambda i: total_copy(i).start())
    over_peers(lambda i: total_copy(i).wait_recv())
    rewards = jnp.sum(jnp.sum(t_all[...], axis=0), axis=0, keepdims=True) / seq
    mean = jnp.sum(rewards, axis=1, keepdims=True) / members_all
    spread = jnp.sum((rewards - mean) ** 2, axis=1, keepdims=True) / members_all
    result = (rewards - mean) / jnp.sqrt(spread + 1e-05)
    for i in range(members_here):
        scores[i] = jnp.sum(jnp.where(lane[0:1] == p * members_here + i, result, 0.0))

    give_gate.wait_send()
    give_up.wait_send()
    give_seeds.wait_send()
    give_prompts.wait_send()
    give_reward.wait_send()
    for link in range(3):
        for index in range(STEPS):
            ring_copy(link, index).wait_send()
    over_peers(lambda i: seed_copy(i).wait_send())
    over_peers(lambda i: part_copy(i).wait_send(), mp_size)
    over_peers(lambda i: total_copy(i).wait_send())


def shards(mp_size, prompts, gate_weight, up_weight, reward_head, member_seeds, counters, member_ranks):
    members_here, seq, width = prompts.shape
    rows, cols = gate_weight.shape
    tokens = members_here * seq
    half = cols // 2
    any_space = pl.BlockSpec(memory_space=pl.ANY)
    vmem = pl.BlockSpec(memory_space=pltpu.VMEM)
    smem = pl.BlockSpec(memory_space=pltpu.SMEM)
    tile_f32 = pltpu.VMEM((8, 128), jnp.float32)
    tile_i32 = pltpu.VMEM((8, 128), jnp.int32)
    dma = pltpu.SemaphoreType.DMA
    return pl.pallas_call(
        functools.partial(kernel, mp_size),
        out_shape=(
            jax.ShapeDtypeStruct((rows, cols), jnp.bfloat16),
            jax.ShapeDtypeStruct((rows, cols), jnp.bfloat16),
            jax.ShapeDtypeStruct((members_here,), jnp.float32),
        ),
        in_specs=[smem, smem, smem, any_space, any_space, any_space, vmem],
        out_specs=(vmem, vmem, smem),
        scratch_shapes=[
            pltpu.VMEM((2 * tokens, width), jnp.bfloat16),
            pltpu.VMEM((2 * GROUP, rows, cols), jnp.bfloat16),
            pltpu.VMEM((2 * tokens, cols), jnp.float32),
            pltpu.VMEM((width, 256), jnp.bfloat16),
            pltpu.VMEM((cols, 256), jnp.bfloat16),
            pltpu.VMEM((16, width), jnp.float32),
            pltpu.VMEM((16, half), jnp.float32),
            pltpu.VMEM((2 * tokens, 128), jnp.float32),
            pltpu.VMEM((2, rows, cols), jnp.bfloat16),
            tile_i32,
            tile_i32,
            tile_i32,
            pltpu.VMEM((GROUP, 8, 128), jnp.int32),
            tile_f32,
            tile_f32,
            tile_f32,
            pltpu.VMEM((mp_size, 8, 128), jnp.float32),
            tile_f32,
            pltpu.VMEM((GROUP, 8, 128), jnp.float32),
            dma((3, STEPS)),
            dma((3, STEPS)),
            dma((5,)),
            dma((5,)),
            dma((GROUP,)),
            dma((GROUP,)),
            dma((2, GROUP)),
            dma((2, GROUP)),
            dma((5,)),
        ],
        compiler_params=pltpu.CompilerParams(
            collective_id=0, has_side_effects=True, vmem_limit_bytes=48 * 1024 * 1024
        ),
        name="generation",
    )(
        member_seeds,
        counters,
        member_ranks,
        prompts.reshape(tokens, width),
        gate_weight,
        up_weight,
        reward_head.reshape(1, cols),
    )


def solution(mesh):
    in_specs = (
        P("pop", None, None),
        P("pop", "mp"),
        P("pop", "mp"),
        P("mp"),
        P("pop"),
        P("pop"),
        P("pop"),
    )
    out_specs = (P("pop", "mp"), P("pop", "mp"), P("pop"))
    body = functools.partial(shards, mesh.shape["mp"])
    return jax.shard_map(body, mesh=mesh, in_specs=in_specs, out_specs=out_specs, check_vma=False)
```

time: 287 us -> 88 us (0.31)
  waiting for transfers between devices: 128 us -> 0 us
  blocking collectives: 114 us -> 0 us
  Pallas kernels: 0 us -> 77.8 us
  matrix products: 20.6 us -> 0 us
  between operations: 16.1 us -> 0.65 us
  local copies, waits for them, and re-layouts: 5.32 us -> 8.47 us
    all_gather x2 -> x0, waiting for transfers between devices: 128 us -> none  [the longest x1 66.5 us: shards(): lax.all_gather(new_up, 'pop', axis=0, tiled=True)]
    unnamed x2 -> x0, blocking collectives: 80 us -> none
    pallas_call x0 -> x1, Pallas kernels: none -> 77.8 us  [shards(): pl.pallas_call(functools.partial(kernel, mp_size), out_shape=(jax.ShapeDt...]
    psum x1 -> x0, blocking collectives: 34.3 us -> none  [shards(): summed = lax.psum(partial_reward, 'mp')]
    dot_general x7 -> x0, matrix products: 20.6 us -> none  [the longest x1 5.99 us: shards(): jnp.dot(flat_rows, lax.all_gather(new_up, 'pop', axis=0, tiled=True), pre...]
    unnamed x12 -> x15, local copies, waits for them, and re-layouts: 4.73 us -> 7.78 us
  transfers between devices with their start and end apart: 2 -> 0, of which waited for: 2 -> 0; matrix products, arithmetic and copies ran while one was open for 5% -> 0% of each run, Pallas kernels for 0% -> 0%
where the time goes in v1:
time: 88 us; the launch traced here: 86.9 us
  Pallas kernels  77.8 us (88%)
  local copies, waits for them, and re-layouts  8.47 us (10%)
    pallas_call x1, Pallas kernels, shards(): pl.pallas_call(functools.partial(kernel, mp_size), out_shape=(jax.ShapeDt...  77.8 us
    unnamed x15, local copies, waits for them, and re-layouts  7.78 us

profile of v1, /device:TPU:1, one launch (start us, length us, event | category | flops | bytes accessed | tf_op | source)
XLA Modules:
  0.0 86.9 jit_solution(17425595566089707603)
XLA Ops:
  0.6 0.7 reshape.13.head
  1.3 0.0 copy-start
  1.3 2.2 %copy-done = bf16[4,128,4096]{2,1,0:T(8,128)(2,1)S(1)} copy-done((bf16[4,128,4096]{2,1,0:T(8,128)(2,1)S(1)}, bf16[4,128,4096]{2,1,0:T(8,128)(2,1)}, u32[]{:S(2)}) %copy-start) | copy-done | bytes 4194328
  3.5 0.0 copy-start.1
  3.5 0.9 %copy-done.1 = bf16[128,512]{1,0:T(8,128)(2,1)S(1)} copy-done((bf16[128,512]{1,0:T(8,128)(2,1)S(1)}, bf16[128,512]{1,0:T(8,128)(2,1)}, u32[]{:S(2)}) %copy-start.1) | copy-done | bytes 131096
  4.4 0.0 copy-start.2
  4.4 0.9 %copy-done.2 = bf16[128,512]{1,0:T(8,128)(2,1)S(1)} copy-done((bf16[128,512]{1,0:T(8,128)(2,1)S(1)}, bf16[128,512]{1,0:T(8,128)(2,1)}, u32[]{:S(2)}) %copy-start.2) | copy-done | bytes 131096
  5.3 0.0 copy-start.3
  5.3 0.7 copy-done.3
  6.0 0.0 copy-start.4
  6.0 0.7 copy-done.4
  6.6 0.0 copy-start.5
  6.6 0.7 copy-done.5
  7.3 77.8 %generation.1 = (bf16[128,512]{1,0:T(8,128)(2,1)S(1)}, bf16[128,512]{1,0:T(8,128)(2,1)S(1)}, f32[4]{0:T(128)S(1)}) custom-call(s32[4]{0:T(128)S(1)} %copy-done.3, s32[4]{0:T(128)S(1)} %copy-done.4, s32[4]{0:T(128)S(1)} %copy-done.5, bf16[512,4096]{1,0:T(8,128)(2,1)S(1)} %bitcast.1, bf16[128,512]{1,0:T(8,128)(2,1)S(1)} %copy-done.1, ...), custom_call_target="tpu_custom_call" | custom-call | tf_op jit(solution)/shard_map/generation/pallas_call | solution.py:403
  85.1 0.7 copy.13
  85.7 0.7 copy.14
  86.4 0.5 copy.15
Async XLA Ops:
  1.3 2.2 %copy-start = (bf16[4,128,4096]{2,1,0:T(8,128)(2,1)S(1)}, bf16[4,128,4096]{2,1,0:T(8,128)(2,1)}, u32[]{:S(2)}) copy-start(bf16[4,128,4096]{2,1,0:T(8,128)(2,1)} %param.7) | copy-start | bytes 12582916
  3.5 0.9 %copy-start.1 = (bf16[128,512]{1,0:T(8,128)(2,1)S(1)}, bf16[128,512]{1,0:T(8,128)(2,1)}, u32[]{:S(2)}) copy-start(bf16[128,512]{1,0:T(8,128)(2,1)} %gate_w.1) | copy-start | bytes 393220
  4.4 0.9 %copy-start.2 = (bf16[128,512]{1,0:T(8,128)(2,1)S(1)}, bf16[128,512]{1,0:T(8,128)(2,1)}, u32[]{:S(2)}) copy-start(bf16[128,512]{1,0:T(8,128)(2,1)} %up_w.1) | copy-start | bytes 393220
  5.3 0.7 copy-start.3
  6.0 0.7 copy-start.4
  6.6 0.7 copy-start.5

commit v2 on v1

--- a/solution.py
+++ b/solution.py
@@ -15,8 +15,8 @@
 GROUP = 16
 
 UP_LINK = [(0, 0, 0), (0, 0, 1), (-1, 0, 0), (0, 1, 1), (-2, 0, 0), (-1, 0, 1), (-3, 0, 0), (-1, 1, 1), (-2, 0, 1), (-2, 1, 1)]
-DOWN_LINK = [(-o, w, 1 - h) for o, w, h in UP_LINK]
-SIDE_LINK = [(0, 0, 1), (0, 0, 0), (-1, 0, 0), (1, 0, 1), (-2, 0, 0), (2, 0, 1), (-3, 0, 0), (3, 0, 1), (-4, 0, 0), (4, 0, 1)]
+DOWN_LINK = [(0, 0, 0), (0, 0, 1), (0, 1, 0), (1, 0, 1), (1, 0, 0), (2, 0, 1), (1, 1, 0), (3, 0, 1), (2, 0, 0), (2, 1, 0)]
+SIDE_LINK = [(0, 0, 0), (0, 0, 1), (-1, 0, 0), (1, 0, 1), (-2, 0, 0), (2, 0, 1), (-3, 0, 0), (3, 0, 1), (-4, 0, 0), (4, 0, 1)]
 SENDS = [UP_LINK, DOWN_LINK, SIDE_LINK]
 ARRIVALS = [
     [(o - 1, w, h) for o, w, h in UP_LINK],
@@ -55,9 +55,9 @@
 def kernel(
     mp_size, seeds, counters, ranks, prompts, gate_w, up_w, head,
     new_gate, new_up, scores,
-    xall, wbuf, acc, lbuf, rbuf, vbuf, cbuf, ubuf, wown,
-    s_own, s_sib, s_chip, s_all, r_own, r_sib, r_part, r_all, t_part, t_all,
-    ring_s, ring_r, one_s, one_r, seed_s, seed_r, red_s, red_r, local_sem,
+    s_seeds, s_counters, s_ranks, v_head, xall, wbuf, acc, zbuf, lbuf, rbuf, vbuf, cbuf, ubuf, wown,
+    s_own, s_sib, s_chip, s_side, s_all, r_own, r_sib, r_part, r_all, t_part, t_all,
+    ring_s, ring_r, one_s, one_r, seed_s, seed_r, red_s, red_r, local_sem, word,
 ):
     rows, cols = gate_w.shape
     half = cols // 2
@@ -86,19 +86,21 @@
     def mp_peer(i):
         return (p, lax.rem(m + i, mp_size))
 
+    ring = min(mp_size, 8)
+    y = lax.rem(m, ring)
+    base = m - y
+    y_up = (p, base + lax.rem(y + 1, ring))
+    y_down = (p, base + lax.rem(y + ring - 1, ring))
+    across = (p, lax.rem(m + ring, mp_size))
+
     barrier = pltpu.get_barrier_semaphore()
-    pl.semaphore_signal(barrier, inc=1, device_id=sibling, device_id_type=MESH)
-
-    def greet(i, carry):
-        pl.semaphore_signal(barrier, inc=1, device_id=chip_peer(i), device_id_type=MESH)
-        return carry
-
-    def greet_mp(i, carry):
-        pl.semaphore_signal(barrier, inc=1, device_id=mp_peer(i), device_id_type=MESH)
-        return carry
-
-    lax.fori_loop(1, GROUP, greet, 0)
-    lax.fori_loop(1, mp_size, greet_mp, 0)
+    near = [sibling, up, down, side, y_up]
+    if ring > 2:
+        near.append(y_down)
+    if mp_size > ring:
+        near.append(across)
+    for device in near:
+        pl.semaphore_signal(barrier, inc=1, device_id=device, device_id_type=MESH)
 
     my_cols = pl.ds(pl.multiple_of(c * half, half), half)
     sib_cols = pl.ds(pl.multiple_of((1 - c) * half, half), half)
@@ -113,17 +115,25 @@
     load_up = pltpu.make_async_copy(up_w, wown.at[1], local_sem.at[4])
     load_gate.start()
     load_up.start()
+    load_head = pltpu.make_async_copy(head, v_head, local_sem.at[5])
+    load_head.start()
+    ints = [(seeds, s_seeds), (counters, s_counters), (ranks, s_ranks)]
+    load_ints = [pltpu.make_async_copy(a, b, local_sem.at[6 + i]) for i, (a, b) in enumerate(ints)]
+    for load in load_ints:
+        load.start()
+    for load in load_ints:
+        load.wait()
 
     lane = lax.broadcasted_iota(jnp.int32, (8, 128), 1)
     sub = lax.broadcasted_iota(jnp.int32, (8, 128), 0)
     block = jnp.zeros((8, 128), jnp.int32)
     for i in range(members_here):
         here = lane == p * members_here + i
-        for row, values in enumerate((seeds, counters, ranks)):
+        for row, values in enumerate((s_seeds, s_counters, s_ranks)):
             block = jnp.where(here & (sub == row), values[i], block)
     s_own[...] = block
 
-    pl.semaphore_wait(barrier, GROUP + mp_size - 1)
+    pl.semaphore_wait(barrier, len(near))
 
     def remote(src, dst, send, recv, device):
         return pltpu.make_async_remote_copy(
@@ -141,7 +151,7 @@
     def ring_copy(link, index):
         offset, other, core = SENDS[link][index]
         column = 1 - xl if other else xl
-        where = pop_of(lax.rem(z + offset + 2 * ZED, ZED), column, core)
+        where = pop_of(lax.rem(z + offset + 2 * ZED, ZED), column, 1 - c if core else c)
         piece = wbuf.at[where]
         return remote(piece, piece, ring_s.at[link, index], ring_r.at[link, index], links[link])
 
@@ -158,19 +168,43 @@
 
     keep_gate.wait()
     keep_up.wait()
+    for link in range(3):
+        ring_copy(link, 0).start()
     give_gate.wait_recv()
     give_up.wait_recv()
-    for index in (0, 1):
-        for link in range(3):
-            ring_copy(link, index).start()
+    for link in range(3):
+        ring_copy(link, 1).start()
     give_prompts.start()
 
     give_seeds.wait_recv()
     s_chip[...] = s_own[...] + s_sib[...]
-    s_all[q] = s_chip[...]
-
-    def seed_copy(i):
-        return remote(s_chip, s_all.at[q], seed_s.at[i], seed_r.at[i], chip_peer(i))
+    give_chip = remote(s_chip, s_side, one_s.at[5], one_r.at[5], side)
+    give_chip.start()
+
+    def seed_hop(step, act):
+        for link, sign in ((0, -1), (1, 1)):
+            if step < ZED // 2 - link:
+                block = s_all.at[lax.rem(z + sign * step + ZED, ZED)]
+                act(remote(block, block, seed_s.at[link, step], seed_r.at[link, step], links[link]))
+
+    def start(copy):
+        copy.start()
+
+    def receive(copy):
+        copy.wait_recv()
+
+    def sent(copy):
+        copy.wait_send()
+
+    def pass_word():
+        pl.semaphore_signal(word.at[0], inc=1, device_id=y_up, device_id_type=MESH)
+        if ring > 2:
+            pl.semaphore_signal(word.at[1], inc=1, device_id=y_down, device_id_type=MESH)
+
+    def take_word():
+        pl.semaphore_wait(word.at[0], 1)
+        if ring > 2:
+            pl.semaphore_wait(word.at[1], 1)
 
     def over_peers(act, count=GROUP):
         def step(i, carry):
@@ -179,13 +213,90 @@
 
         lax.fori_loop(1, count, step, 0)
 
-    over_peers(lambda i: seed_copy(i).start())
+    def hash_members():
+        pick = lane == q * 8 + sub
+        columns = [
+            jnp.sum(
+                jnp.where(pick, anchor_of(s_chip[0:1, :], s_chip[1:2, :] + 1, slot), 0), axis=1, keepdims=True
+            )
+            for slot in range(4)
+        ]
+        wide = lax.broadcasted_iota(jnp.int32, (8, 1024), 1)
+        for start in range(0, width, 1024):
+            vbuf[0:8, start : start + 1024] = stream(columns[0], wide + start)
+            vbuf[8:16, start : start + 1024] = stream(columns[2], wide + start)
+        here = m * cols + c * half + lax.broadcasted_iota(jnp.int32, (8, half), 1)
+        cbuf[0:8, :] = stream(columns[1], here) * SIGMA
+        cbuf[8:16, :] = stream(columns[3], here) * SIGMA
+
+    n_chunks = 4
+    chunk = width // n_chunks
+
+    def project(i):
+        k = pl.ds(i * chunk, chunk)
+        own = lax.dot_general(
+            xall[:, k], vbuf[:, k].astype(jnp.bfloat16), (((1,), (1,)), ((), ())), preferred_element_type=jnp.float32
+        )
+        ubuf[:, 0:16] = own if i == 0 else ubuf[:, 0:16] + own
+
+    seq = 2 * tokens // 8
+
+    def rank_one():
+        for i in range(8):
+            r = slice(i * seq, (i + 1) * seq)
+            for index in range(2):
+                s = slice(index * half, (index + 1) * half)
+                j = index * 8 + i
+                acc[r, s] += ubuf[r, j : j + 1] * cbuf[j : j + 1, :]
+
+    def multiply(offset, other=None, core=None):
+        zz = lax.rem(z + offset + ZED, ZED)
+        if other is None:
+            first, count = pop_of(zz, 0, 0), 4
+        elif core is None:
+            first, count = pop_of(zz, 1 - xl if other else xl, 0), 2
+        else:
+            first, count = pop_of(zz, 1 - xl if other else xl, 1 - c if core else c), 1
+        depth = count * rows
+        k = pl.ds(pl.multiple_of(first * rows, depth), depth)
+        w = wbuf[pl.ds(first, count)].reshape(depth, cols)
+        acc[...] += jnp.dot(xall[:, k], w, preferred_element_type=jnp.float32)
 
     acc[...] = jnp.zeros_like(acc)
+    pass_word()
+    hash_members()
     arrive(0)
-    over_peers(lambda i: seed_copy(i).wait_recv())
+    take_word()
+    give_chip.wait_recv()
+    s_all[z] = s_chip[...] + s_side[...]
+    seed_hop(0, start)
+    pass_word()
+    arrive(1)
+    take_word()
+    seed_hop(0, receive)
+    seed_hop(1, start)
+    pass_word()
+    own_prompts.wait()
+    arrive(2)
+    take_word()
+    seed_hop(1, receive)
+    seed_hop(2, start)
+    pass_word()
+    give_prompts.wait_recv()
+    project(0)
+    project(1)
+    multiply(0)
+    arrive(3)
+    take_word()
+    seed_hop(2, receive)
+    seed_hop(3, start)
+    project(2)
+    project(3)
+    multiply(-1)
+    arrive(4)
+    seed_hop(3, receive)
     table = s_all[0]
-    for i in range(1, GROUP):
+    for i in range(1, ZED):
         table = table + s_all[i]
     seed_row = table[0:1, :]
     count_row = table[1:2, :]
@@ -227,109 +338,38 @@
             )
             out[...] = (wown[index].astype(jnp.float32) + scaling * delta).astype(out.dtype)
 
-    def hash_members():
-        pick = lane == q * 8 + sub
-        columns = [
-            jnp.sum(
-                jnp.where(pick, anchor_of(seed_row, count_row + 1, slot), 0), axis=1, keepdims=True
-            )
-            for slot in range(4)
-        ]
-        wide = lax.broadcasted_iota(jnp.int32, (8, 1024), 1)
-        for start in range(0, width, 1024):
-            vbuf[0:8, start : start + 1024] = stream(columns[0], wide + start)
-            vbuf[8:16, start : start + 1024] = stream(columns[2], wide + start)
-        here = m * cols + c * half + lax.broadcasted_iota(jnp.int32, (8, half), 1)
-        cbuf[0:8, :] = stream(columns[1], here) * SIGMA
-        cbuf[8:16, :] = stream(columns[3], here) * SIGMA
-
-    tile = 256
-    n_tiles = 2 * tokens // tile
-
-    def project():
-        def step(i, carry):
-            r = pl.ds(pl.multiple_of(i * tile, tile), tile)
-            own = lax.dot_general(
-                xall[r, :], vbuf[...].astype(jnp.bfloat16), (((1,), (1,)), ((), ())),
+    def low_rank(i):
+        k = pl.ds(i * chunk, chunk)
+        own = jnp.dot(xall[:, k], lbuf[k, :], preferred_element_type=jnp.float32)
+        zbuf[...] = own if i == 0 else zbuf[...] + own
+
+    def add_low_rank():
+        for index in range(2):
+            part = slice(index * 128, index * 128 + 128)
+            acc[:, index * half : (index + 1) * half] += lax.dot_general(
+                (zbuf[:, part] * scaling).astype(jnp.bfloat16),
+                rbuf[pl.ds(pl.multiple_of(c * half, half), half), part],
+                (((1,), (1,)), ((), ())),
                 preferred_element_type=jnp.float32,
             )
-            ubuf[r, 0:16] = own
-            return carry
-
-        lax.fori_loop(0, n_tiles, step, 0)
-
-    def low_rank():
-        def step(i, carry):
-            r = pl.ds(pl.multiple_of(i * tile, tile), tile)
-            zl = jnp.dot(xall[r, :], lbuf[...], preferred_element_type=jnp.float32) * scaling
-            zl = zl.astype(jnp.bfloat16)
-            for index in range(2):
-                part = slice(index * 128, index * 128 + 128)
-                acc[r, index * half : (index + 1) * half] += lax.dot_general(
-                    zl[:, part],
-                    rbuf[pl.ds(pl.multiple_of(c * half, half), half), part],
-                    (((1,), (1,)), ((), ())),
-                    preferred_element_type=jnp.float32,
-                )
-            return carry
-
-        lax.fori_loop(0, n_tiles, step, 0)
-
-    seq = 2 * tokens // 8
-
-    def rank_one():
-        for i in range(8):
-            r = slice(i * seq, (i + 1) * seq)
-            for index in range(2):
-                s = slice(index * half, (index + 1) * half)
-                j = index * 8 + i
-                acc[r, s] += ubuf[r, j : j + 1] * cbuf[j : j + 1, :]
-
-    def multiply(offset, other, core=None):
-        zz = lax.rem(z + offset + ZED, ZED)
-        column = 1 - xl if other else xl
-        first = pop_of(zz, column, core or 0)
-        depth = rows if core is not None else 2 * rows
-        k = pl.ds(pl.multiple_of(first * rows, rows), depth)
-        w_of = (lambda: wbuf[first]) if core is not None else (lambda: wbuf[pl.ds(first, 2)].reshape(depth, cols))
-
-        def step(i, carry):
-            r = pl.ds(pl.multiple_of(i * tile, tile), tile)
-            acc[r, :] += jnp.dot(xall[r, k], w_of(), preferred_element_type=jnp.float32)
-            return carry
-
-        lax.fori_loop(0, n_tiles, step, 0)
-
-    hash_left(0, 8)
-    arrive(1)
-    hash_left(8, 10)
-    own_prompts.wait()
-    give_prompts.wait_recv()
-    arrive(2)
-    hash_left(18, 14)
-    arrive(3)
+
+    n_hash = width // 128
+    hash_left(0, n_hash // 2)
+    multiply(1)
+    arrive(5)
+    hash_left(n_hash // 2, n_hash // 2)
     hash_right()
+    arrive(6)
+    for i in range(n_chunks):
+        low_rank(i)
+    arrive(7)
     fresh_rows()
-    hash_members()
-    arrive(4)
-    low_rank()
-    arrive(5)
-    project()
+    add_low_rank()
     rank_one()
-    arrive(6)
-    multiply(0, 0)
-    multiply(0, 1)
-    multiply(-1, 0)
-    multiply(1, 0)
-    arrive(7)
-    multiply(-1, 1)
-    multiply(1, 1)
-    multiply(-2, 0)
-    multiply(2, 0)
+    multiply(2)
     multiply(4, 0)
     arrive(8)
-    multiply(-2, 1)
-    multiply(2, 1)
+    multiply(-2)
     multiply(-3, 0)
     multiply(3, 0)
     multiply(-3, 1, 0)
@@ -340,7 +380,8 @@
     multiply(3, 1, 0)
     multiply(4, 1, 1)
 
-    head_row = head[:, my_cols].astype(jnp.float32)
+    load_head.wait()
+    head_row = v_head[my_cols].astype(jnp.float32).reshape(1, half)
     parts = []
     for i in range(8):
         r = slice(i * seq, (i + 1) * seq)
@@ -384,9 +425,17 @@
     for link in range(3):
         for index in range(STEPS):
             ring_copy(link, index).wait_send()
-    over_peers(lambda i: seed_copy(i).wait_send())
+    give_chip.wait_send()
+    for step in range(ZED // 2):
+        seed_hop(step, sent)
     over_peers(lambda i: part_copy(i).wait_send(), mp_size)
     over_peers(lambda i: total_copy(i).wait_send())
+
+
+def finish(*refs):
+    count = len(refs) // 2
+    for source, target in zip(refs[:count], refs[count:]):
+        target[...] = source[...]
 
 
 def shards(mp_size, prompts, gate_weight, up_weight, reward_head, member_seeds, counters, member_ranks):
@@ -394,25 +443,30 @@
     rows, cols = gate_weight.shape
     tokens = members_here * seq
     half = cols // 2
-    any_space = pl.BlockSpec(memory_space=pl.ANY)
+    hbm = pl.BlockSpec(memory_space=pltpu.HBM)
     vmem = pl.BlockSpec(memory_space=pltpu.VMEM)
     smem = pl.BlockSpec(memory_space=pltpu.SMEM)
     tile_f32 = pltpu.VMEM((8, 128), jnp.float32)
     tile_i32 = pltpu.VMEM((8, 128), jnp.int32)
     dma = pltpu.SemaphoreType.DMA
-    return pl.pallas_call(
+    results = pl.pallas_call(
         functools.partial(kernel, mp_size),
         out_shape=(
             jax.ShapeDtypeStruct((rows, cols), jnp.bfloat16),
             jax.ShapeDtypeStruct((rows, cols), jnp.bfloat16),
             jax.ShapeDtypeStruct((members_here,), jnp.float32),
         ),
-        in_specs=[smem, smem, smem, any_space, any_space, any_space, vmem],
+        in_specs=[hbm] * 7,
         out_specs=(vmem, vmem, smem),
         scratch_shapes=[
+            pltpu.SMEM((members_here,), jnp.int32),
+            pltpu.SMEM((members_here,), jnp.int32),
+            pltpu.SMEM((members_here,), jnp.int32),
+            pltpu.VMEM((cols,), jnp.bfloat16),
             pltpu.VMEM((2 * tokens, width), jnp.bfloat16),
             pltpu.VMEM((2 * GROUP, rows, cols), jnp.bfloat16),
             pltpu.VMEM((2 * tokens, cols), jnp.float32),
+            pltpu.VMEM((2 * tokens, 256), jnp.float32),
             pltpu.VMEM((width, 256), jnp.bfloat16),
             pltpu.VMEM((cols, 256), jnp.bfloat16),
             pltpu.VMEM((16, width), jnp.float32),
@@ -422,7 +476,8 @@
             tile_i32,
             tile_i32,
             tile_i32,
-            pltpu.VMEM((GROUP, 8, 128), jnp.int32),
+            tile_i32,
+            pltpu.VMEM((ZED, 8, 128), jnp.int32),
             tile_f32,
             tile_f32,
             tile_f32,
@@ -431,16 +486,17 @@
             pltpu.VMEM((GROUP, 8, 128), jnp.float32),
             dma((3, STEPS)),
             dma((3, STEPS)),
-            dma((5,)),
-            dma((5,)),
-            dma((GROUP,)),
-            dma((GROUP,)),
+            dma((6,)),
+            dma((6,)),
+            dma((2, ZED // 2)),
+            dma((2, ZED // 2)),
             dma((2, GROUP)),
             dma((2, GROUP)),
-            dma((5,)),
+            dma((9,)),
+            pltpu.SemaphoreType.REGULAR((2,)),
         ],
         compiler_params=pltpu.CompilerParams(
-            collective_id=0, has_side_effects=True, vmem_limit_bytes=48 * 1024 * 1024
+            collective_id=0, has_side_effects=True, vmem_limit_bytes=60 * 1024 * 1024
         ),
         name="generation",
     )(
@@ -450,8 +506,16 @@
         prompts.reshape(tokens, width),
         gate_weight,
         up_weight,
-        reward_head.reshape(1, cols),
+        reward_head,
     )
+    return pl.pallas_call(
+        finish,
+        out_shape=tuple(jax.ShapeDtypeStruct(r.shape, r.dtype) for r in results),
+        in_specs=[vmem] * 3,
+        out_specs=(vmem,) * 3,
+        compiler_params=pltpu.CompilerParams(vmem_limit_bytes=60 * 1024 * 1024),
+        name="finish",
+    )(*results)
 
 
 def solution(mesh):

time: 88 us -> 69.6 us (0.79); the launches traced: 86.9 us -> 69.4 us
  Pallas kernels: 77.8 us -> 68.8 us
  local copies, waits for them, and re-layouts: 8.47 us -> 0 us
    pallas_call x1, Pallas kernels: 77.8 us -> 67.1 us  [shards(): pl.pallas_call(functools.partial(kernel, mp_size), out_shape=(jax.ShapeDt...]
    unnamed x15 -> x0, local copies, waits for them, and re-layouts: 7.78 us -> none
    pallas_call x0 -> x1, Pallas kernels: none -> 1.68 us  [shards(): pl.pallas_call(finish, out_shape=tuple((jax.ShapeDtypeStruct(r.shape, r.d...]
where the time goes in v2:
time: 69.6 us; the launch traced here: 69.4 us
  Pallas kernels  68.8 us (99%)
    pallas_call x1, Pallas kernels, shards(): pl.pallas_call(functools.partial(kernel, mp_size), out_shape=(jax.ShapeDt...  67.1 us
    pallas_call x1, Pallas kernels, shards(): pl.pallas_call(finish, out_shape=tuple((jax.ShapeDtypeStruct(r.shape, r.d...  1.68 us

profile of v2, /device:TPU:1, one launch (start us, length us, event | category | flops | bytes accessed | tf_op | source)
XLA Modules:
  0.0 69.4 jit_solution(12962861515009650402)
XLA Ops:
  0.6 67.1 %generation.1 = (bf16[128,512]{1,0:T(8,128)(2,1)}, bf16[128,512]{1,0:T(8,128)(2,1)}, f32[4]{0:T(128)}) custom-call(s32[4]{0:T(128)} %seeds.1, s32[4]{0:T(128)} %counters.1, s32[4]{0:T(128)} %ranks.1, bf16[512,4096]{1,0:T(8,128)(2,1)} %bitcast.1, bf16[128,512]{1,0:T(8,128)(2,1)} %gate_w.1, bf16[128,512]{1,0:T(8,128)(2,1)} %up_w.1, bf16[512]{0:T(512)(128)(2,1)} %head.1), custom_call_target="tpu_custom_call" | custom-call | tf_op jit(solution)/shard_map/generation/pallas_call | solution.py:452
  67.7 1.7 %finish.1 = (bf16[128,512]{1,0:T(8,128)(2,1)}, bf16[128,512]{1,0:T(8,128)(2,1)}, f32[4]{0:T(128)}) custom-call(bf16[128,512]{1,0:T(8,128)(2,1)} %get-tuple-element.6.refs_0_, bf16[128,512]{1,0:T(8,128)(2,1)} %get-tuple-element.7.refs_1_, f32[4]{0:T(128)} %get-tuple-element.8.refs_2_), custom_call_target="tpu_custom_call" | custom-call | tf_op jit(solution)/shard_map/finish/pallas_call | solution.py:511

commit v3 on v2

--- a/solution.py
+++ b/solution.py
@@ -55,7 +55,7 @@
 def kernel(
     mp_size, seeds, counters, ranks, prompts, gate_w, up_w, head,
     new_gate, new_up, scores,
-    s_seeds, s_counters, s_ranks, v_head, xall, wbuf, acc, zbuf, lbuf, rbuf, vbuf, cbuf, ubuf, wown,
+    s_seeds, s_counters, s_ranks, v_head, xall, wbuf, acc, z_own, z_sib, lbuf, lown, rbuf, vbuf, cbuf, wown,
     s_own, s_sib, s_chip, s_side, s_all, r_own, r_sib, r_part, r_all, t_part, t_all,
     ring_s, ring_r, one_s, one_r, seed_s, seed_r, red_s, red_r, local_sem, word,
 ):
@@ -80,11 +80,15 @@
     side = (pop_of(z, 1 - xl, c), m)
     links = [up, down, side]
 
+    def by_distance(count, sides):
+        pairs = [(o, w) for o in range(count) for w in range(sides) if o or w]
+        return sorted(pairs, key=lambda pair: -min(pair[0], count - pair[0]))
+
+    chip_pairs = by_distance(ZED, 2)
+
     def chip_peer(i):
-        return (2 * lax.rem(q + i, GROUP) + c, m)
-
-    def mp_peer(i):
-        return (p, lax.rem(m + i, mp_size))
+        o, w = chip_pairs[i]
+        return (pop_of(lax.rem(z + o, ZED), 1 - xl if w else xl, c), m)
 
     ring = min(mp_size, 8)
     y = lax.rem(m, ring)
@@ -92,6 +96,12 @@
     y_up = (p, base + lax.rem(y + 1, ring))
     y_down = (p, base + lax.rem(y + ring - 1, ring))
     across = (p, lax.rem(m + ring, mp_size))
+
+    mp_pairs = by_distance(ring, mp_size // ring)
+
+    def mp_peer(i):
+        o, w = mp_pairs[i]
+        return (p, lax.rem((base + ring if w else base), mp_size) + lax.rem(y + o, ring))
 
     barrier = pltpu.get_barrier_semaphore()
     near = [sibling, up, down, side, y_up]
@@ -206,12 +216,11 @@
         if ring > 2:
             pl.semaphore_wait(word.at[1], 1)
 
-    def over_peers(act, count=GROUP):
-        def step(i, carry):
-            act(i)
-            return carry
-
-        lax.fori_loop(1, count, step, 0)
+    n_chunks = 2
+    chunk = width // 2 // n_chunks
+
+    def width_part(i):
+        return pl.ds(pl.multiple_of((c * n_chunks + i) * chunk, chunk), chunk)
 
     def hash_members():
         pick = lane == q * 8 + sub
@@ -221,23 +230,23 @@
             )
             for slot in range(4)
         ]
-        wide = lax.broadcasted_iota(jnp.int32, (8, 1024), 1)
-        for start in range(0, width, 1024):
-            vbuf[0:8, start : start + 1024] = stream(columns[0], wide + start)
-            vbuf[8:16, start : start + 1024] = stream(columns[2], wide + start)
+        wide = lax.broadcasted_iota(jnp.int32, (8, chunk), 1)
+        for i in range(n_chunks):
+            first = (c * n_chunks + i) * chunk
+            vbuf[0:8, i * chunk : (i + 1) * chunk] = stream(columns[0], wide + first)
+            vbuf[8:16, i * chunk : (i + 1) * chunk] = stream(columns[2], wide + first)
         here = m * cols + c * half + lax.broadcasted_iota(jnp.int32, (8, half), 1)
         cbuf[0:8, :] = stream(columns[1], here) * SIGMA
         cbuf[8:16, :] = stream(columns[3], here) * SIGMA
 
-    n_chunks = 4
-    chunk = width // n_chunks
-
     def project(i):
-        k = pl.ds(i * chunk, chunk)
         own = lax.dot_general(
-            xall[:, k], vbuf[:, k].astype(jnp.bfloat16), (((1,), (1,)), ((), ())), preferred_element_type=jnp.float32
+            xall[:, width_part(i)],
+            vbuf[:, i * chunk : (i + 1) * chunk].astype(jnp.bfloat16),
+            (((1,), (1,)), ((), ())),
+            preferred_element_type=jnp.float32,
         )
-        ubuf[:, 0:16] = own if i == 0 else ubuf[:, 0:16] + own
+        z_own[:, 256:272] = own if i == 0 else z_own[:, 256:272] + own
 
     seq = 2 * tokens // 8
 
@@ -247,16 +256,26 @@
             for index in range(2):
                 s = slice(index * half, (index + 1) * half)
                 j = index * 8 + i
-                acc[r, s] += ubuf[r, j : j + 1] * cbuf[j : j + 1, :]
-
-    def multiply(offset, other=None, core=None):
+                along = z_own[r, 256 + j : 257 + j] + z_sib[r, 256 + j : 257 + j]
+                acc[r, s] += along * cbuf[j : j + 1, :]
+
+    def block_of(offset, other, core):
+        zz = lax.rem(z + offset + ZED, ZED)
+        return pop_of(zz, 1 - xl if other else xl, 1 - c if core else c)
+
+    def multiply(*pieces):
+        firsts = [block_of(*piece) for piece in pieces]
+        ks = [pl.ds(pl.multiple_of(first * rows, rows), rows) for first in firsts]
+        x = jnp.concatenate([xall[:, k] for k in ks], axis=1) if len(ks) > 1 else xall[:, ks[0]]
+        w = jnp.concatenate([wbuf[first] for first in firsts], axis=0) if len(ks) > 1 else wbuf[firsts[0]]
+        acc[...] += jnp.dot(x, w, preferred_element_type=jnp.float32)
+
+    def multiply_chip(offset, other=None):
         zz = lax.rem(z + offset + ZED, ZED)
         if other is None:
             first, count = pop_of(zz, 0, 0), 4
-        elif core is None:
+        else:
             first, count = pop_of(zz, 1 - xl if other else xl, 0), 2
-        else:
-            first, count = pop_of(zz, 1 - xl if other else xl, 1 - c if core else c), 1
         depth = count * rows
         k = pl.ds(pl.multiple_of(first * rows, depth), depth)
         w = wbuf[pl.ds(first, count)].reshape(depth, cols)
@@ -284,15 +303,13 @@
     pass_word()
     give_prompts.wait_recv()
     project(0)
-    project(1)
-    multiply(0)
+    multiply_chip(0)
     arrive(3)
     take_word()
     seed_hop(2, receive)
     seed_hop(3, start)
-    project(2)
-    project(3)
-    multiply(-1)
+    project(1)
+    multiply_chip(-1)
     arrive(4)
     seed_hop(3, receive)
     table = s_all[0]
@@ -307,12 +324,14 @@
     right_up = anchor_of(seed_row, count_row, 3)
     scaling = RATE / (members_all * SIGMA)
 
-    def hash_left(first, count):
+    def hash_left(row, target, start):
+        position = row + lax.broadcasted_iota(jnp.int32, (128, 128), 0)
+        target[pl.ds(start, 128), 0:128] = (stream(left_gate, position) * fit_row).astype(jnp.bfloat16)
+        target[pl.ds(start, 128), 128:256] = (stream(left_up, position) * fit_row).astype(jnp.bfloat16)
+
+    def hash_width(first, count):
         def step(i, carry):
-            start = pl.multiple_of(i * 128, 128)
-            position = start + lax.broadcasted_iota(jnp.int32, (128, 128), 0)
-            lbuf[pl.ds(start, 128), 0:128] = (stream(left_gate, position) * fit_row).astype(jnp.bfloat16)
-            lbuf[pl.ds(start, 128), 128:256] = (stream(left_up, position) * fit_row).astype(jnp.bfloat16)
+            hash_left(c * (width // 2) + i * 128, lbuf, pl.multiple_of(i * 128, 128))
             return carry
 
         lax.fori_loop(first, first + count, step, 0)
@@ -328,57 +347,54 @@
         lax.fori_loop(0, cols // 128, step, 0)
 
     def fresh_rows():
-        own = pl.ds(pl.multiple_of(p * rows, rows), rows)
+        hash_left(p * rows, lown, 0)
         load_gate.wait()
         load_up.wait()
         for index, out in enumerate((new_gate, new_up)):
             part = pl.ds(index * 128, 128)
             delta = lax.dot_general(
-                lbuf[own, part], rbuf[:, part], (((1,), (1,)), ((), ())), preferred_element_type=jnp.float32
+                lown[:, part], rbuf[:, part], (((1,), (1,)), ((), ())), preferred_element_type=jnp.float32
             )
             out[...] = (wown[index].astype(jnp.float32) + scaling * delta).astype(out.dtype)
 
     def low_rank(i):
-        k = pl.ds(i * chunk, chunk)
-        own = jnp.dot(xall[:, k], lbuf[k, :], preferred_element_type=jnp.float32)
-        zbuf[...] = own if i == 0 else zbuf[...] + own
+        own = jnp.dot(xall[:, width_part(i)], lbuf[i * chunk : (i + 1) * chunk, :], preferred_element_type=jnp.float32)
+        z_own[:, 0:256] = own if i == 0 else z_own[:, 0:256] + own
 
     def add_low_rank():
         for index in range(2):
             part = slice(index * 128, index * 128 + 128)
             acc[:, index * half : (index + 1) * half] += lax.dot_general(
-                (zbuf[:, part] * scaling).astype(jnp.bfloat16),
+                ((z_own[:, part] + z_sib[:, part]) * scaling).astype(jnp.bfloat16),
                 rbuf[pl.ds(pl.multiple_of(c * half, half), half), part],
                 (((1,), (1,)), ((), ())),
                 preferred_element_type=jnp.float32,
             )
 
-    n_hash = width // 128
-    hash_left(0, n_hash // 2)
-    multiply(1)
+    give_low = remote(z_own, z_sib, one_s.at[6], one_r.at[6], sibling)
+    n_hash = width // 2 // 128
+    hash_width(0, n_hash)
     arrive(5)
-    hash_left(n_hash // 2, n_hash // 2)
-    hash_right()
-    arrive(6)
     for i in range(n_chunks):
         low_rank(i)
+    give_low.start()
+    multiply_chip(1)
+    arrive(6)
+    hash_right()
+    fresh_rows()
+    give_low.wait_recv()
+    add_low_rank()
     arrive(7)
-    fresh_rows()
-    add_low_rank()
     rank_one()
-    multiply(2)
-    multiply(4, 0)
+    multiply_chip(2)
+    multiply_chip(4, 0)
     arrive(8)
-    multiply(-2)
-    multiply(-3, 0)
-    multiply(3, 0)
-    multiply(-3, 1, 0)
-    multiply(3, 1, 1)
-    multiply(-4, 1, 0)
+    multiply_chip(-2)
+    multiply_chip(-3, 0)
+    multiply_chip(3, 0)
+    multiply((-3, 1, 0), (3, 1, 1), (4, 1, 0))
     arrive(9)
-    multiply(-3, 1, 1)
-    multiply(3, 1, 0)
-    multiply(4, 1, 1)
+    multiply((-3, 1, 1), (3, 1, 0), (4, 1, 1))
 
     load_head.wait()
     head_row = v_head[my_cols].astype(jnp.float32).reshape(1, half)
@@ -400,22 +416,25 @@
     def part_copy(i):
         return remote(r_part, r_all.at[m], red_s.at[0, i], red_r.at[0, i], mp_peer(i))
 
-    over_peers(lambda i: part_copy(i).start(), mp_size)
-    over_peers(lambda i: part_copy(i).wait_recv(), mp_size)
+    for i in range(len(mp_pairs)):
+        part_copy(i).start()
+    for i in range(len(mp_pairs)):
+        part_copy(i).wait_recv()
     t_part[...] = jnp.sum(r_all[...], axis=0)
     t_all[q] = t_part[...]
 
     def total_copy(i):
         return remote(t_part, t_all.at[q], red_s.at[1, i], red_r.at[1, i], chip_peer(i))
 
-    over_peers(lambda i: total_copy(i).start())
-    over_peers(lambda i: total_copy(i).wait_recv())
+    for i in range(len(chip_pairs)):
+        total_copy(i).start()
+    for i in range(len(chip_pairs)):
+        total_copy(i).wait_recv()
     rewards = jnp.sum(jnp.sum(t_all[...], axis=0), axis=0, keepdims=True) / seq
     mean = jnp.sum(rewards, axis=1, keepdims=True) / members_all
     spread = jnp.sum((rewards - mean) ** 2, axis=1, keepdims=True) / members_all
     result = (rewards - mean) / jnp.sqrt(spread + 1e-05)
-    for i in range(members_here):
-        scores[i] = jnp.sum(jnp.where(lane[0:1] == p * members_here + i, result, 0.0))
+    scores[...] = jnp.broadcast_to(result, scores.shape)
 
     give_gate.wait_send()
     give_up.wait_send()
@@ -426,16 +445,23 @@
         for index in range(STEPS):
             ring_copy(link, index).wait_send()
     give_chip.wait_send()
+    give_low.wait_send()
     for step in range(ZED // 2):
         seed_hop(step, sent)
-    over_peers(lambda i: part_copy(i).wait_send(), mp_size)
-    over_peers(lambda i: total_copy(i).wait_send())
-
-
-def finish(*refs):
-    count = len(refs) // 2
-    for source, target in zip(refs[:count], refs[count:]):
-        target[...] = source[...]
+    for i in range(len(mp_pairs)):
+        part_copy(i).wait_send()
+    for i in range(len(chip_pairs)):
+        total_copy(i).wait_send()
+
+
+def finish(gate, up, all_scores, new_gate, new_up, scores):
+    new_gate[...] = gate[...]
+    new_up[...] = up[...]
+    first = lax.axis_index("pop") * scores.shape[0]
+    lane = lax.broadcasted_iota(jnp.int32, all_scores.shape, 1)
+    sub = lax.broadcasted_iota(jnp.int32, all_scores.shape, 0)
+    for i in range(scores.shape[0]):
+        scores[i] = jnp.sum(jnp.where((lane == first + i) & (sub == 0), all_scores[...], 0.0))
 
 
 def shards(mp_size, prompts, gate_weight, up_weight, reward_head, member_seeds, counters, member_ranks):
@@ -452,12 +478,12 @@
     results = pl.pallas_call(
         functools.partial(kernel, mp_size),
         out_shape=(
-            jax.ShapeDtypeStruct((rows, cols), jnp.bfloat16),
-            jax.ShapeDtypeStruct((rows, cols), jnp.bfloat16),
-            jax.ShapeDtypeStruct((members_here,), jnp.float32),
+            pltpu.VMEM((rows, cols), jnp.bfloat16),
+            pltpu.VMEM((rows, cols), jnp.bfloat16),
+            pltpu.VMEM((8, 128), jnp.float32),
         ),
         in_specs=[hbm] * 7,
-        out_specs=(vmem, vmem, smem),
+        out_specs=(vmem,) * 3,
         scratch_shapes=[
             pltpu.SMEM((members_here,), jnp.int32),
             pltpu.SMEM((members_here,), jnp.int32),
@@ -466,12 +492,13 @@
             pltpu.VMEM((2 * tokens, width), jnp.bfloat16),
             pltpu.VMEM((2 * GROUP, rows, cols), jnp.bfloat16),
             pltpu.VMEM((2 * tokens, cols), jnp.float32),
-            pltpu.VMEM((2 * tokens, 256), jnp.float32),
-            pltpu.VMEM((width, 256), jnp.bfloat16),
+            pltpu.VMEM((2 * tokens, 384), jnp.float32),
+            pltpu.VMEM((2 * tokens, 384), jnp.float32),
+            pltpu.VMEM((width // 2, 256), jnp.bfloat16),
+            pltpu.VMEM((rows, 256), jnp.bfloat16),
             pltpu.VMEM((cols, 256), jnp.bfloat16),
-            pltpu.VMEM((16, width), jnp.float32),
+            pltpu.VMEM((16, width // 2), jnp.float32),
             pltpu.VMEM((16, half), jnp.float32),
-            pltpu.VMEM((2 * tokens, 128), jnp.float32),
             pltpu.VMEM((2, rows, cols), jnp.bfloat16),
             tile_i32,
             tile_i32,
@@ -486,8 +513,8 @@
             pltpu.VMEM((GROUP, 8, 128), jnp.float32),
             dma((3, STEPS)),
             dma((3, STEPS)),
-            dma((6,)),
-            dma((6,)),
+            dma((7,)),
+            dma((7,)),
             dma((2, ZED // 2)),
             dma((2, ZED // 2)),
             dma((2, GROUP)),
@@ -510,10 +537,14 @@
     )
     return pl.pallas_call(
         finish,
-        out_shape=tuple(jax.ShapeDtypeStruct(r.shape, r.dtype) for r in results),
+        out_shape=(
+            jax.ShapeDtypeStruct((rows, cols), jnp.bfloat16),
+            jax.ShapeDtypeStruct((rows, cols), jnp.bfloat16),
+            jax.ShapeDtypeStruct((members_here,), jnp.float32),
+        ),
         in_specs=[vmem] * 3,
-        out_specs=(vmem,) * 3,
-        compiler_params=pltpu.CompilerParams(vmem_limit_bytes=60 * 1024 * 1024),
+        out_specs=(vmem, vmem, smem),
+        compiler_params=pltpu.CompilerParams(vmem_limit_bytes=8 * 1024 * 1024),
         name="finish",
     )(*results)
 

time: 69.6 us -> 64.5 us (0.927)
  Pallas kernels: 68.8 us -> 63.8 us
    pallas_call x2, Pallas kernels: 68.8 us -> 63.8 us  [the longest x1 63.1 us: shards(): pl.pallas_call(functools.partial(kernel, mp_size), out_shape=(pltpu.VMEM(...]
where the time goes in v3:
time: 64.5 us; the launch traced here: 64.4 us
  Pallas kernels  63.8 us (99%)
    pallas_call x1, Pallas kernels, shards(): pl.pallas_call(functools.partial(kernel, mp_size), out_shape=(pltpu.VMEM(...  63.1 us

profile of v3, /device:TPU:1, one launch (start us, length us, event | category | flops | bytes accessed | tf_op | source)
XLA Modules:
  0.0 64.4 jit_solution(436830216591301072)
XLA Ops:
  0.6 63.1 %generation.1 = (bf16[128,512]{1,0:T(8,128)(2,1)S(1)}, bf16[128,512]{1,0:T(8,128)(2,1)S(1)}, f32[8,128]{1,0:T(8,128)S(1)}) custom-call(s32[4]{0:T(128)} %seeds.1, s32[4]{0:T(128)} %counters.1, s32[4]{0:T(128)} %ranks.1, bf16[512,4096]{1,0:T(8,128)(2,1)} %bitcast.1, bf16[128,512]{1,0:T(8,128)(2,1)} %gate_w.1, bf16[128,512]{1,0:T(8,128)(2,1)} %up_w.1, ...), custom_call_target="tpu_custom_call" | custom-call | tf_op jit(solution)/shard_map/generation/pallas_call | solution.py:478
  63.7 0.7 %finish.1 = (bf16[128,512]{1,0:T(8,128)(2,1)}, bf16[128,512]{1,0:T(8,128)(2,1)}, f32[4]{0:T(128)}) custom-call(bf16[128,512]{1,0:T(8,128)(2,1)S(1)} %get-tuple-element.6.gate, bf16[128,512]{1,0:T(8,128)(2,1)S(1)} %get-tuple-element.7.up, f32[8,128]{1,0:T(8,128)S(1)} %get-tuple-element.8.all_scores), custom_call_target="tpu_custom_call" | custom-call | tf_op jit(solution)/shard_map/finish/pallas_call | solution.py:538

commit v4 on v3

--- a/solution.py
+++ b/solution.py
@@ -55,7 +55,7 @@
 def kernel(
     mp_size, seeds, counters, ranks, prompts, gate_w, up_w, head,
     new_gate, new_up, scores,
-    s_seeds, s_counters, s_ranks, v_head, xall, wbuf, acc, z_own, z_sib, lbuf, lown, rbuf, vbuf, cbuf, wown,
+    s_seeds, s_counters, s_ranks, v_head, xall, wbuf, acc, z_own, z_sib, u_own, u_sib, lbuf, lown, rbuf, vbuf, cbuf, wown,
     s_own, s_sib, s_chip, s_side, s_all, r_own, r_sib, r_part, r_all, t_part, t_all,
     ring_s, ring_r, one_s, one_r, seed_s, seed_r, red_s, red_r, local_sem, word,
 ):
@@ -246,7 +246,7 @@
             (((1,), (1,)), ((), ())),
             preferred_element_type=jnp.float32,
         )
-        z_own[:, 256:272] = own if i == 0 else z_own[:, 256:272] + own
+        u_own[:, 0:16] = own if i == 0 else u_own[:, 0:16] + own
 
     seq = 2 * tokens // 8
 
@@ -256,7 +256,7 @@
             for index in range(2):
                 s = slice(index * half, (index + 1) * half)
                 j = index * 8 + i
-                along = z_own[r, 256 + j : 257 + j] + z_sib[r, 256 + j : 257 + j]
+                along = u_own[r, j : j + 1] + u_sib[r, j : j + 1]
                 acc[r, s] += along * cbuf[j : j + 1, :]
 
     def block_of(offset, other, core):
@@ -281,7 +281,9 @@
         w = wbuf[pl.ds(first, count)].reshape(depth, cols)
         acc[...] += jnp.dot(xall[:, k], w, preferred_element_type=jnp.float32)
 
+    give_along = remote(u_own, u_sib, one_s.at[4], one_r.at[4], sibling)
     acc[...] = jnp.zeros_like(acc)
+    u_own[...] = jnp.zeros_like(u_own)
     pass_word()
     hash_members()
     arrive(0)
@@ -309,6 +311,7 @@
     seed_hop(2, receive)
     seed_hop(3, start)
     project(1)
+    give_along.start()
     multiply_chip(-1)
     arrive(4)
     seed_hop(3, receive)
@@ -359,7 +362,7 @@
 
     def low_rank(i):
         own = jnp.dot(xall[:, width_part(i)], lbuf[i * chunk : (i + 1) * chunk, :], preferred_element_type=jnp.float32)
-        z_own[:, 0:256] = own if i == 0 else z_own[:, 0:256] + own
+        z_own[...] = own if i == 0 else z_own[...] + own
 
     def add_low_rank():
         for index in range(2):
@@ -382,12 +385,13 @@
     arrive(6)
     hash_right()
     fresh_rows()
+    give_along.wait_recv()
+    rank_one()
+    arrive(7)
+    multiply_chip(2)
+    multiply_chip(4, 0)
     give_low.wait_recv()
     add_low_rank()
-    arrive(7)
-    rank_one()
-    multiply_chip(2)
-    multiply_chip(4, 0)
     arrive(8)
     multiply_chip(-2)
     multiply_chip(-3, 0)
@@ -407,7 +411,7 @@
     summed = jnp.sum(jnp.concatenate(parts, axis=0) * head_row, axis=1, keepdims=True)
     r_own[...] = jnp.where(lane == q * 8 + sub, summed, 0.0)
 
-    give_reward = remote(r_own, r_sib, one_s.at[4], one_r.at[4], sibling)
+    give_reward = remote(r_own, r_sib, one_s.at[7], one_r.at[7], sibling)
     give_reward.start()
     give_reward.wait_recv()
     r_part[...] = r_own[...] + r_sib[...]
@@ -446,6 +450,7 @@
             ring_copy(link, index).wait_send()
     give_chip.wait_send()
     give_low.wait_send()
+    give_along.wait_send()
     for step in range(ZED // 2):
         seed_hop(step, sent)
     for i in range(len(mp_pairs)):
@@ -492,8 +497,10 @@
             pltpu.VMEM((2 * tokens, width), jnp.bfloat16),
             pltpu.VMEM((2 * GROUP, rows, cols), jnp.bfloat16),
             pltpu.VMEM((2 * tokens, cols), jnp.float32),
-            pltpu.VMEM((2 * tokens, 384), jnp.float32),
-            pltpu.VMEM((2 * tokens, 384), jnp.float32),
+            pltpu.VMEM((2 * tokens, 256), jnp.float32),
+            pltpu.VMEM((2 * tokens, 256), jnp.float32),
+            pltpu.VMEM((2 * tokens, 128), jnp.float32),
+            pltpu.VMEM((2 * tokens, 128), jnp.float32),
             pltpu.VMEM((width // 2, 256), jnp.bfloat16),
             pltpu.VMEM((rows, 256), jnp.bfloat16),
             pltpu.VMEM((cols, 256), jnp.bfloat16),
@@ -513,8 +520,8 @@
             pltpu.VMEM((GROUP, 8, 128), jnp.float32),
             dma((3, STEPS)),
             dma((3, STEPS)),
-            dma((7,)),
-            dma((7,)),
+            dma((8,)),
+            dma((8,)),
             dma((2, ZED // 2)),
             dma((2, ZED // 2)),
             dma((2, GROUP)),

time: 64.5 us -> 64 us (level)
  no operation moved by 1% of the time
where the time goes in v4:
time: 64 us; the launch traced here: 63.9 us
  Pallas kernels  63.3 us (99%)
  between operations  0.64 us (1%)
    pallas_call x1, Pallas kernels, shards(): pl.pallas_call(functools.partial(kernel, mp_size), out_shape=(pltpu.VMEM(...  62.6 us

profile of v4, /device:TPU:1, one launch (start us, length us, event | category | flops | bytes accessed | tf_op | source)
XLA Modules:
  0.0 63.9 jit_solution(9398872864244296725)
XLA Ops:
  0.6 62.6 %generation.1 = (bf16[128,512]{1,0:T(8,128)(2,1)S(1)}, bf16[128,512]{1,0:T(8,128)(2,1)S(1)}, f32[8,128]{1,0:T(8,128)S(1)}) custom-call(s32[4]{0:T(128)} %seeds.1, s32[4]{0:T(128)} %counters.1, s32[4]{0:T(128)} %ranks.1, bf16[512,4096]{1,0:T(8,128)(2,1)} %bitcast.1, bf16[128,512]{1,0:T(8,128)(2,1)} %gate_w.1, bf16[128,512]{1,0:T(8,128)(2,1)} %up_w.1, ...), custom_call_target="tpu_custom_call" | custom-call | tf_op jit(solution)/shard_map/generation/pallas_call | solution.py:483
  63.2 0.7 %finish.1 = (bf16[128,512]{1,0:T(8,128)(2,1)}, bf16[128,512]{1,0:T(8,128)(2,1)}, f32[4]{0:T(128)}) custom-call(bf16[128,512]{1,0:T(8,128)(2,1)S(1)} %get-tuple-element.6.gate, bf16[128,512]{1,0:T(8,128)(2,1)S(1)} %get-tuple-element.7.up, f32[8,128]{1,0:T(8,128)S(1)} %get-tuple-element.8.all_scores), custom_call_target="tpu_custom_call" | custom-call | tf_op jit(solution)/shard_map/finish/pallas_call | solution.py:545

commit v5 on v4

--- a/solution.py
+++ b/solution.py
@@ -131,9 +131,49 @@
     load_ints = [pltpu.make_async_copy(a, b, local_sem.at[6 + i]) for i, (a, b) in enumerate(ints)]
     for load in load_ints:
         load.start()
+
+    pl.semaphore_wait(barrier, len(near))
+
+    def remote(src, dst, send, recv, device):
+        return pltpu.make_async_remote_copy(
+            src_ref=src, dst_ref=dst, send_sem=send, recv_sem=recv, device_id=device, device_id_type=MESH
+        )
+
+    give_gate = remote(gate_w.at[:, sib_cols], wbuf.at[p, :, pl.ds(0, half)], one_s.at[0], one_r.at[0], sibling)
+    give_up = remote(up_w.at[:, sib_cols], wbuf.at[p, :, pl.ds(half, half)], one_s.at[1], one_r.at[1], sibling)
+    give_seeds = remote(s_own, s_sib, one_s.at[2], one_r.at[2], sibling)
+    give_prompts = remote(prompts, xall.at[own_rows], one_s.at[3], one_r.at[3], sibling)
+    give_gate.start()
+    give_up.start()
+
+    def ring_copy(link, index):
+        offset, other, core = SENDS[link][index]
+        column = 1 - xl if other else xl
+        where = pop_of(lax.rem(z + offset + 2 * ZED, ZED), column, 1 - c if core else c)
+        piece = wbuf.at[where]
+        return remote(piece, piece, ring_s.at[link, index], ring_r.at[link, index], links[link])
+
+    def pass_on(piece):
+        for link in range(3):
+            for index, sent in enumerate(SENDS[link]):
+                if same_piece(piece, sent):
+                    ring_copy(link, index).start()
+
+    def arrive(step):
+        for link in range(3):
+            ring_copy(link, step).wait_recv()
+            pass_on(ARRIVALS[link][step])
+
+    keep_gate.wait()
+    keep_up.wait()
+    for link in range(3):
+        ring_copy(link, 0).start()
+    give_gate.wait_recv()
+    give_up.wait_recv()
+    for link in range(3):
+        ring_copy(link, 1).start()
     for load in load_ints:
         load.wait()
-
     lane = lax.broadcasted_iota(jnp.int32, (8, 128), 1)
     sub = lax.broadcasted_iota(jnp.int32, (8, 128), 0)
     block = jnp.zeros((8, 128), jnp.int32)
@@ -142,48 +182,7 @@
         for row, values in enumerate((s_seeds, s_counters, s_ranks)):
             block = jnp.where(here & (sub == row), values[i], block)
     s_own[...] = block
-
-    pl.semaphore_wait(barrier, len(near))
-
-    def remote(src, dst, send, recv, device):
-        return pltpu.make_async_remote_copy(
-            src_ref=src, dst_ref=dst, send_sem=send, recv_sem=recv, device_id=device, device_id_type=MESH
-        )
-
-    give_gate = remote(gate_w.at[:, sib_cols], wbuf.at[p, :, pl.ds(0, half)], one_s.at[0], one_r.at[0], sibling)
-    give_up = remote(up_w.at[:, sib_cols], wbuf.at[p, :, pl.ds(half, half)], one_s.at[1], one_r.at[1], sibling)
-    give_seeds = remote(s_own, s_sib, one_s.at[2], one_r.at[2], sibling)
-    give_prompts = remote(prompts, xall.at[own_rows], one_s.at[3], one_r.at[3], sibling)
-    give_gate.start()
-    give_up.start()
     give_seeds.start()
-
-    def ring_copy(link, index):
-        offset, other, core = SENDS[link][index]
-        column = 1 - xl if other else xl
-        where = pop_of(lax.rem(z + offset + 2 * ZED, ZED), column, 1 - c if core else c)
-        piece = wbuf.at[where]
-        return remote(piece, piece, ring_s.at[link, index], ring_r.at[link, index], links[link])
-
-    def pass_on(piece):
-        for link in range(3):
-            for index, sent in enumerate(SENDS[link]):
-                if same_piece(piece, sent):
-                    ring_copy(link, index).start()
-
-    def arrive(step):
-        for link in range(3):
-            ring_copy(link, step).wait_recv()
-            pass_on(ARRIVALS[link][step])
-
-    keep_gate.wait()
-    keep_up.wait()
-    for link in range(3):
-        ring_copy(link, 0).start()
-    give_gate.wait_recv()
-    give_up.wait_recv()
-    for link in range(3):
-        ring_copy(link, 1).start()
     give_prompts.start()
 
     give_seeds.wait_recv()
@@ -270,15 +269,14 @@
         w = jnp.concatenate([wbuf[first] for first in firsts], axis=0) if len(ks) > 1 else wbuf[firsts[0]]
         acc[...] += jnp.dot(x, w, preferred_element_type=jnp.float32)
 
-    def multiply_chip(offset, other=None):
-        zz = lax.rem(z + offset + ZED, ZED)
-        if other is None:
-            first, count = pop_of(zz, 0, 0), 4
-        else:
-            first, count = pop_of(zz, 1 - xl if other else xl, 0), 2
-        depth = count * rows
+    def whole(offset, other):
+        return (offset, other, 0), (offset, other, 1)
+
+    def multiply_chip(offset):
+        first = pop_of(lax.rem(z + offset + ZED, ZED), 0, 0)
+        depth = 4 * rows
         k = pl.ds(pl.multiple_of(first * rows, depth), depth)
-        w = wbuf[pl.ds(first, count)].reshape(depth, cols)
+        w = wbuf[pl.ds(first, 4)].reshape(depth, cols)
         acc[...] += jnp.dot(xall[:, k], w, preferred_element_type=jnp.float32)
 
     give_along = remote(u_own, u_sib, one_s.at[4], one_r.at[4], sibling)
@@ -388,15 +386,11 @@
     give_along.wait_recv()
     rank_one()
     arrive(7)
-    multiply_chip(2)
-    multiply_chip(4, 0)
+    multiply(*whole(2, 0), *whole(2, 1), *whole(4, 0), *whole(-2, 0))
     give_low.wait_recv()
     add_low_rank()
     arrive(8)
-    multiply_chip(-2)
-    multiply_chip(-3, 0)
-    multiply_chip(3, 0)
-    multiply((-3, 1, 0), (3, 1, 1), (4, 1, 0))
+    multiply(*whole(-2, 1), (-3, 1, 0), (3, 1, 1), *whole(-3, 0), *whole(3, 0), (4, 1, 0))
     arrive(9)
     multiply((-3, 1, 1), (3, 1, 0), (4, 1, 1))
 

time: 64 us -> 63.9 us (level)
  no operation moved by 1% of the time
where the time goes in v5:
time: 63.9 us; the launch traced here: 63.8 us
  Pallas kernels  63.2 us (99%)
  between operations  0.64 us (1%)
    pallas_call x1, Pallas kernels, shards(): pl.pallas_call(functools.partial(kernel, mp_size), out_shape=(pltpu.VMEM(...  62.5 us

profile of v5, /device:TPU:1, one launch (start us, length us, event | category | flops | bytes accessed | tf_op | source)
XLA Modules:
  0.0 63.8 jit_solution(1568122512968543417)
XLA Ops:
  0.6 62.5 %generation.1 = (bf16[128,512]{1,0:T(8,128)(2,1)S(1)}, bf16[128,512]{1,0:T(8,128)(2,1)S(1)}, f32[8,128]{1,0:T(8,128)S(1)}) custom-call(s32[4]{0:T(128)} %seeds.1, s32[4]{0:T(128)} %counters.1, s32[4]{0:T(128)} %ranks.1, bf16[512,4096]{1,0:T(8,128)(2,1)} %bitcast.1, bf16[128,512]{1,0:T(8,128)(2,1)} %gate_w.1, bf16[128,512]{1,0:T(8,128)(2,1)} %up_w.1, ...), custom_call_target="tpu_custom_call" | custom-call | tf_op jit(solution)/shard_map/generation/pallas_call | solution.py:477
  63.1 0.7 %finish.1 = (bf16[128,512]{1,0:T(8,128)(2,1)}, bf16[128,512]{1,0:T(8,128)(2,1)}, f32[4]{0:T(128)}) custom-call(bf16[128,512]{1,0:T(8,128)(2,1)S(1)} %get-tuple-element.6.gate, bf16[128,512]{1,0:T(8,128)(2,1)S(1)} %get-tuple-element.7.up, f32[8,128]{1,0:T(8,128)S(1)} %get-tuple-element.8.all_scores), custom_call_target="tpu_custom_call" | custom-call | tf_op jit(solution)/shard_map/finish/pallas_call | solution.py:539
